TPU v7x, 32 devices: a whole 2x2x4 slice. The times are simulated.
32 devices in a mesh: group: 4 (over y, x), row: 8 (over z, core).
Axes of the slice: x: 2, y: 2, z: 4, core: 2. Of those that a mesh axis runs over, the one named last changes fastest.
Arguments:
- snapshots: bfloat16 [1024, 8192], P(('group', 'row')), may hold values from -6 to 6
- bnd_index: int32 [16, 1024], replicated, may hold values from 0 to 8191
- recovery: bfloat16 [512, 512, 1024], P(('group', 'row')), may hold values from -0.1875 to 0.1875
- block_se: int32 [512], P(('group', 'row')), may hold values from 0 to 3
- connect: int32 [16384, 24], P(('group', 'row')), may hold values from 0 to 8703, as said below
- stress_mat: bfloat16 [16384, 6, 24], P(('group', 'row')), may hold values from -1.25 to 1.25
Outputs:
- stresses: bfloat16 [16384, 6, 1024], P(('group', 'row'))
Inputs may be any that keep to these rules, and one draw needn't show every extreme that they name: `connect`: among one device's elements, the first 8192 entries of its connectivity, read element by element, name each of rows 256 to 8447 once.
All inputs are finite; a program needn't handle non-finite values.
Results may differ from a plain program's by a relative error of at most 0.0049.
Values may be sent and summed in bfloat16 or wider, within the bound.
No kernel may reach another device: no remote copies, remote signals or barrier semaphores. Data moves between devices by JAX's collectives and lax.ppermute only.
A program may use at most 128 MiB of HBM per device.

v0:
```python
import math
import jax
import jax.numpy as jnp
from jax import lax
from jax.sharding import PartitionSpec as P

HW = 256
NC = 6
NDOF = 24


def extended_2(cells, sides, width):
    for axis, dim in sides:
        count = lax.axis_size(axis)
        ends = count - 1
        head = lax.slice_in_dim(cells, 0, width, axis=dim)
        tail = lax.slice_in_dim(cells, cells.shape[dim] - width, cells.shape[dim], axis=dim)
        cells = jnp.concatenate(
            [
                lax.ppermute(tail, axis, [(i, (i + 1) % count) for i in range(ends)]),
                cells,
                lax.ppermute(head, axis, [((i + 1) % count, i) for i in range(ends)]),
            ],
            axis=dim,
        )
    return cells


def body(snapshots, bnd_index, recovery, block_se, connect, stress_mat):
    picked = jnp.take(snapshots, bnd_index, axis=1)
    widened = lax.all_gather(picked, "row", axis=0, tiled=True)
    arrived = lax.all_to_all(widened, "group", split_axis=1, concat_axis=0, tiled=True)
    bvals = jnp.transpose(arrived, (1, 0, 2))

    def one_block(entry):
        matrix, which = entry
        sliced = lax.dynamic_index_in_dim(bvals, which, 0, keepdims=False)
        result = lax.dot_general(
            matrix, sliced, (((1,), (1,)), ((), ())), preferred_element_type=jnp.float32
        )
        return result.astype(jnp.bfloat16)

    interior = lax.map(one_block, (recovery, block_se))
    interior = interior.reshape(interior.shape[0] * interior.shape[1], interior.shape[2])
    extended = extended_2(interior, (("row", 0),), HW)
    elem_count = connect.shape[0]
    elem_block = math.gcd(elem_count, 128)

    def one_part(entry):
        link_rows, mat_rows = entry
        values = jnp.take(extended, link_rows, axis=0)
        result = jnp.einsum("eck,ekt->ect", mat_rows, values, preferred_element_type=jnp.float32)
        return result.astype(jnp.bfloat16)

    links = connect.reshape(elem_count // elem_block, elem_block, NDOF)
    mats = stress_mat.reshape(elem_count // elem_block, elem_block, NC, NDOF)
    stresses = lax.map(one_part, (links, mats))
    return stresses.reshape(elem_count, NC, extended.shape[1])


def solution(mesh):
    in_specs = (
        P(("group", "row"), None),
        P(),
        P(("group", "row"), None, None),
        P(("group", "row")),
        P(("group", "row"), None),
        P(("group", "row"), None, None),
    )
    out_specs = P(("group", "row"), None, None)
    return jax.shard_map(body, mesh=mesh, in_specs=in_specs, out_specs=out_specs, check_vma=False)
```

profile of v0, /device:TPU:1, one launch (start us, length us, event | category | flops | bytes accessed | tf_op | source)
XLA Modules:
  0.0 552.2 jit_solution(11753239106156816748)
XLA Ops:
  10.2 57.9 %gather_fusion.1 = bf16[16384,32]{1,0:T(8,128)(2,1)} fusion(bf16[32,8192]{0,1:T(8,128)(2,1)S(1)} %copy.25, s32[16384]{0:T(1024)S(1)} %broadcast_clamp_fusion.1), kind=kCustom, calls=%fused_computation.1 | custom fusion | bytes 2162688 | tf_op jit(solution)/shard_map/jit(_take)/gather | solution.py:30
  73.2 84.7 %all-gather.2.cloned.1.call-done = bf16[256,16,1024]{2,1,0:T(8,128)(2,1)} async-done(((bf16[32,16,1024]{2,1,0:T(8,128)(2,1)}), bf16[256,16,1024]{2,1,0:T(8,128)(2,1)}) %all-gather.2.cloned.1.call-update) | async-done | bytes 8388624 | tf_op jit(solution)/shard_map/all_gather | solution.py:31
  157.9 11.3 %copy.27 = bf16[256,16,1024]{2,0,1:T(8,128)(2,1)} copy(bf16[256,16,1024]{2,1,0:T(8,128)(2,1)} %all-gather.2.cloned.1.call-done) | data formatting | bytes 16777216 | tf_op jit(solution)/shard_map/all_gather | solution.py:31
  169.2 5.7 %all-to-all-start = ((bf16[256,16,1024]{2,0,1:T(8,128)(2,1)}), bf16[256,16,1024]{2,0,1:T(8,128)(2,1)}, u32[]{:S(2)}, u32[]{:S(2)}) async-start(bf16[256,16,1024]{2,0,1:T(8,128)(2,1)} %copy.27), calls=%async_computation | async-start | bytes 16777216 | tf_op jit(solution)/shard_map/all_to_all | solution.py:32
  174.9 92.2 %all-to-all-done = bf16[256,16,1024]{2,0,1:T(8,128)(2,1)} async-done(((bf16[256,16,1024]{2,0,1:T(8,128)(2,1)}), bf16[256,16,1024]{2,0,1:T(8,128)(2,1)}, u32[]{:S(2)}, u32[]{:S(2)}) %all-to-all-start) | async-done | bytes 8388640 | tf_op jit(solution)/shard_map/all_to_all | solution.py:32
  267.1 8.0 %copy.28 = bf16[4,256,4,1024]{3,1,0,2:T(8,128)(2,1)} copy(bf16[4,256,4,1024]{3,1,2,0:T(8,128)(2,1)} %bitcast.14) | data formatting | bytes 16777216 | tf_op jit(solution)/shard_map/all_to_all | solution.py:32
  275.1 111.2 %while.20 = (s32[]{:T(128)}, bf16[16,512,1024]{2,1,0:T(8,128)(2,1)}, bf16[16,512,1024]{2,1,0:T(8,128)(2,1)}, s32[16]{0:T(128)S(1)}, bf16[4,1024,1024]{2,1,0:T(8,128)(2,1)}, /*index=5*/s32[]{:T(128)}, s32[]{:T(128)}, s32[]{:T(128)}) while((s32[]{:T(128)}, bf16[16,512,1024]{2,1,0:T(8,128)(2,1)}, bf16[16,512,1024]{2,1,0:T(8,128)(2,1)}, ...), condition=%wide.region_1.2_spmd, body=%wide.region_0.1_spmd.sunk | while | flops 1074266112 | bytes 4195463 | solution.py:43
  277.8 4.2 fusion.34
  291.7 4.2 fusion.34
  319.4 4.2 fusion.34
  326.4 4.3 fusion.34
  354.2 4.3 fusion.34
  382.0 4.2 fusion.34
  395.5 4.4 collective-permute-done.1
  399.9 22.7 %pad_maximum_fusion = bf16[8704,1024]{1,0:T(8,128)(2,1)} fusion(bf16[256,1024]{1,0:T(8,128)(2,1)S(1)} %collective-permute-done.1, bf16[8192,1024]{1,0:T(8,128)(2,1)} %bitcast.67, bf16[256,1024]{1,0:T(8,128)(2,1)S(1)} %collective-permute-done), kind=kLoop, calls=%fused_computation.25 | loop fusion | flops 53477376 | bytes 35651584 | tf_op jit(solution)/shard_map/concatenate | solution.py:18
  422.6 122.7 %while.21 = (s32[]{:T(128)}, bf16[4,128,6,1024]{3,1,0,2:T(8,128)(2,1)}, bf16[4,128,6,24]{3,2,1,0:T(8,128)(2,1)S(1)}, s32[4,128,24]{2,1,0:T(8,128)S(1)}, bf16[8704,1024]{1,0:T(8,128)(2,1)}, /*index=5*/s32[]{:T(128)}) while((s32[]{:T(128)}, bf16[4,128,6,1024]{3,1,0,2:T(8,128)(2,1)}, bf16[4,128,6,24]{3,2,1,0:T(8,128)(2,1)S(1)}, ...), condition=%wide.region_3.4_spmd, body=%wide.region_2.3_spmd.sunk | while | flops 41711616 | bytes 23973456 | solution.py:57
  422.8 24.3 %gather_fusion = bf16[3072,1024]{1,0:T(8,128)(2,1)} fusion(bf16[8704,1024]{1,0:T(8,128)(2,1)} %get-tuple-element.185, s32[3072]{0:T(1024)S(1)} %broadcast_clamp_fusion.3), kind=kCustom, calls=%fused_computation.clone.1 | custom fusion | bytes 12595200 | tf_op jit(solution)/shard_map/while/body/eval_jaxpr/jit(_take)/gather | solution.py:51
  447.1 4.2 convert_bitcast_fusion.2
  453.4 24.3 %gather_fusion = bf16[3072,1024]{1,0:T(8,128)(2,1)} fusion(bf16[8704,1024]{1,0:T(8,128)(2,1)} %get-tuple-element.185, s32[3072]{0:T(1024)S(1)} %broadcast_clamp_fusion.3), kind=kCustom, calls=%fused_computation.clone.1 | custom fusion | bytes 12595200 | tf_op jit(solution)/shard_map/while/body/eval_jaxpr/jit(_take)/gather | solution.py:51
  477.7 4.2 convert_bitcast_fusion.2
  484.1 24.3 %gather_fusion = bf16[3072,1024]{1,0:T(8,128)(2,1)} fusion(bf16[8704,1024]{1,0:T(8,128)(2,1)} %get-tuple-element.185, s32[3072]{0:T(1024)S(1)} %broadcast_clamp_fusion.3), kind=kCustom, calls=%fused_computation.clone.1 | custom fusion | bytes 12595200 | tf_op jit(solution)/shard_map/while/body/eval_jaxpr/jit(_take)/gather | solution.py:51
  508.4 4.2 convert_bitcast_fusion.2
  514.8 24.3 %gather_fusion = bf16[3072,1024]{1,0:T(8,128)(2,1)} fusion(bf16[8704,1024]{1,0:T(8,128)(2,1)} %get-tuple-element.185, s32[3072]{0:T(1024)S(1)} %broadcast_clamp_fusion.3), kind=kCustom, calls=%fused_computation.clone.1 | custom fusion | bytes 12595200 | tf_op jit(solution)/shard_map/while/body/eval_jaxpr/jit(_take)/gather | solution.py:51
  539.1 4.2 convert_bitcast_fusion.2
  (69 shorter events, 79.1 us)
Async XLA Ops:
  6.5 151.4 %all-gather.2.cloned.1.call-start = ((), (), s32[]{:S(2)}) async-start(), calls=%async_computation.1 | async-start | bytes 9437184 | tf_op jit(solution)/shard_map/all_gather | solution.py:31
  169.2 97.9 %all-to-all-start = ((bf16[256,16,1024]{2,0,1:T(8,128)(2,1)}), bf16[256,16,1024]{2,0,1:T(8,128)(2,1)}, u32[]{:S(2)}, u32[]{:S(2)}) async-start(bf16[256,16,1024]{2,0,1:T(8,128)(2,1)} %copy.27), calls=%async_computation | async-start | bytes 16777216 | tf_op jit(solution)/shard_map/all_to_all | solution.py:32
  267.1 8.0 %copy-start.2 = (s32[16]{0:T(128)S(1)}, s32[16]{0:T(128)}, u32[]{:S(2)}) copy-start(s32[16]{0:T(128)} %param.13) | copy-start | bytes 196
  275.0 117.0 %copy-start = (bf16[512,6,24]{0,2,1:T(8,128)(2,1)S(1)}, bf16[512,6,24]{0,2,1:T(8,128)(2,1)}, u32[]{:S(2)}) copy-start(bf16[512,6,24]{0,2,1:T(8,128)(2,1)} %param.15) | copy-start | bytes 442372
  275.1 117.8 %copy-start.1 = (s32[512,24]{0,1:T(8,128)S(1)}, s32[512,24]{0,1:T(8,128)}, u32[]{:S(2)}) copy-start(s32[512,24]{0,1:T(8,128)} %param.14) | copy-start | bytes 147460
  387.5 8.0 %collective-permute-start = (bf16[256,1024]{1,0:T(8,128)(2,1)S(1)}, bf16[256,1024]{1,0:T(8,128)(2,1)S(1)}, u32[]{:S(2)}, u32[]{:S(2)}) collective-permute-start(bf16[256,1024]{1,0:T(8,128)(2,1)S(1)} %get-tuple-element.81), channel_id=1, source_target_pairs={{0,1},{1,2},{2,3},{3,4},{4,5},{5,6},{6,7},{8,9},{9,10},{10,11},{11... | collective-permute-start | bytes 1572872 | tf_op jit(solution)/shard_map/ppermute | solution.py:20
  389.4 10.5 %collective-permute-start.1 = (bf16[256,1024]{1,0:T(8,128)(2,1)S(1)}, bf16[256,1024]{1,0:T(8,128)(2,1)S(1)}, u32[]{:S(2)}, u32[]{:S(2)}) collective-permute-start(bf16[256,1024]{1,0:T(8,128)(2,1)S(1)} %get-tuple-element.82), channel_id=1, source_target_pairs={{1,0},{2,1},{3,2},{4,3},{5,4},{6,5},{7,6},{9,8},{10,9},{11,10},{12... | collective-permute-start | bytes 1572872 | tf_op jit(solution)/shard_map/ppermute | solution.py:22
Sparse Core Ops, SparseCore 0:
  73.3 84.5 all-gather.1
where the time goes:
time: 554 us; the launch traced here: 552 us
  local copies, waits for them, and re-layouts  201 us (36%)
  waiting for transfers between devices  184 us (33%)
  matrix products  84.3 us (15%)
  loops' own time  33.3 us (6%)
  other arithmetic  25.7 us (5%)
  between operations  13.5 us (2%)
  starting transfers between devices  10.2 us (2%)
    gather x4, local copies, waits for them, and re-layouts, one_part(): values = jnp.take(extended, link_rows, axis=0)  97.1 us
    all_to_all x1, waiting for transfers between devices, body(): lax.all_to_all(widened, 'group', split_axis=1, concat_axis=0, tiled=True)  92.2 us
    all_gather x1, waiting for transfers between devices, body(): widened = lax.all_gather(picked, 'row', axis=0, tiled=True)  84.7 us
    dot_general x16, matrix products, one_block(): lax.dot_general(matrix, sliced, (((1,), (1,)), ((), ())), preferred_eleme...  67.4 us
    gather x2, local copies, waits for them, and re-layouts, body(): picked = jnp.take(snapshots, bnd_index, axis=1)  61.9 us
    another operation x1, loops' own time, body(): interior = lax.map(one_block, (recovery, block_se))  33.2 us
    concatenate x1, other arithmetic, extended_2(): jnp.concatenate([lax.ppermute(tail, axis, [(i, (i + 1) % count) for i in...  22.7 us
    dot_general x4, matrix products, one_part(): jnp.einsum('eck,ekt->ect', mat_rows, values, preferred_element_type=jnp.f...  16.9 us
  transfers between devices with their start and end apart: 4, of which 4 were waited for; matrix products, arithmetic and copies ran while one was open for 0% of the time, Pallas kernels for 0%

commit v1 on v0

--- a/solution.py
+++ b/solution.py
@@ -7,6 +7,22 @@
 HW = 256
 NC = 6
 NDOF = 24
+
+
+def ring_gather(x, axis, dim):
+    ways, here, step = (lax.axis_size(axis), lax.axis_index(axis), x.shape[dim])
+    shape = [n * ways if d == dim else n for d, n in enumerate(x.shape)]
+    full = lax.dynamic_update_slice_in_dim(jnp.zeros(shape, x.dtype), x, here * step, axis=dim)
+    going_up = going_down = x
+    for far in range(1, ways // 2 + 1):
+        going_up = lax.ppermute(going_up, axis, [(d, (d + 1) % ways) for d in range(ways)])
+        full = lax.dynamic_update_slice_in_dim(full, going_up, (here - far) % ways * step, axis=dim)
+        if 2 * far < ways:
+            going_down = lax.ppermute(going_down, axis, [(d, (d - 1) % ways) for d in range(ways)])
+            full = lax.dynamic_update_slice_in_dim(
+                full, going_down, (here + far) % ways * step, axis=dim
+            )
+    return full
 
 
 def extended_2(cells, sides, width):
@@ -28,7 +44,7 @@
 
 def body(snapshots, bnd_index, recovery, block_se, connect, stress_mat):
     picked = jnp.take(snapshots, bnd_index, axis=1)
-    widened = lax.all_gather(picked, "row", axis=0, tiled=True)
+    widened = ring_gather(picked, "row", 0)
     arrived = lax.all_to_all(widened, "group", split_axis=1, concat_axis=0, tiled=True)
     bvals = jnp.transpose(arrived, (1, 0, 2))
 

time: 554 us -> 531 us (0.958)
  waiting for transfers between devices: 184 us -> 162 us
  between operations: 13.5 us -> 0.13 us
  starting transfers between devices: 10.2 us -> 22.5 us
  loops' own time: 33.3 us -> 26.5 us
    all_gather x1 -> x0, waiting for transfers between devices: 84.7 us -> none  [body(): widened = lax.all_gather(picked, 'row', axis=0, tiled=True)]
    ppermute x0 -> x7, waiting for transfers between devices: none -> 62.3 us  [the longest x4 54.9 us: ring_gather(): lax.ppermute(going_up, axis, [(d, (d + 1) % ways) for d in range(ways)])]
    dynamic_update_slice x0 -> x7, local copies, waits for them, and re-layouts: none -> 12.6 us  [the longest x4 6.86 us: ring_gather(): lax.dynamic_update_slice_in_dim(full, going_up, (here - far) % ways * ste...]
    all_gather x1 -> x0, local copies, waits for them, and re-layouts: 11.3 us -> none  [body(): widened = lax.all_gather(picked, 'row', axis=0, tiled=True)]
    ppermute x0 -> x7, starting transfers between devices: none -> 10.2 us  [the longest x4 10.2 us: ring_gather(): lax.ppermute(going_up, axis, [(d, (d + 1) % ways) for d in range(ways)])]
    another operation x1, loops' own time: 33.2 us -> 26.4 us  [body(): interior = lax.map(one_block, (recovery, block_se))]
  transfers between devices with their start and end apart: 4 -> 10, of which waited for: 4 -> 10; matrix products, arithmetic and copies ran while one was open for 0% -> 2% of each run, Pallas kernels for 0% -> 0%
where the time goes in v1:
time: 531 us; the launch traced here: 526 us
  local copies, waits for them, and re-layouts  205 us (39%)
  waiting for transfers between devices  162 us (31%)
  matrix products  84.3 us (16%)
  loops' own time  26.5 us (5%)
  other arithmetic  25.9 us (5%)
  starting transfers between devices  22.5 us (4%)
    gather x4, local copies, waits for them, and re-layouts, one_part(): values = jnp.take(extended, link_rows, axis=0)  97.3 us
    all_to_all x1, waiting for transfers between devices, body(): lax.all_to_all(widened, 'group', split_axis=1, concat_axis=0, tiled=True)  91.8 us
    dot_general x16, matrix products, one_block(): lax.dot_general(matrix, sliced, (((1,), (1,)), ((), ())), preferred_eleme...  67.4 us
    gather x2, local copies, waits for them, and re-layouts, body(): picked = jnp.take(snapshots, bnd_index, axis=1)  61.4 us
    ppermute x4, waiting for transfers between devices, ring_gather(): lax.ppermute(going_up, axis, [(d, (d + 1) % ways) for d in range(ways)])  54.9 us
    another operation x1, loops' own time, body(): interior = lax.map(one_block, (recovery, block_se))  26.4 us
    concatenate x1, other arithmetic, extended_2(): jnp.concatenate([lax.ppermute(tail, axis, [(i, (i + 1) % count) for i in...  22.8 us
    dot_general x4, matrix products, one_part(): jnp.einsum('eck,ekt->ect', mat_rows, values, preferred_element_type=jnp.f...  16.9 us
  transfers between devices with their start and end apart: 10, of which 10 were waited for; matrix products, arithmetic and copies ran while one was open for 2% of the time, Pallas kernels for 0%

profile of v1, /device:TPU:1, one launch (start us, length us, event | category | flops | bytes accessed | tf_op | source)
XLA Modules:
  0.0 525.9 jit_solution(12030857701186819668)
XLA Ops:
  3.7 57.9 %gather_fusion.1 = bf16[16384,32]{1,0:T(8,128)(2,1)} fusion(bf16[32,8192]{0,1:T(8,128)(2,1)S(1)} %copy.18, s32[16384]{0:T(1024)S(1)} %broadcast_clamp_fusion.1), kind=kCustom, calls=%fused_computation.1 | custom fusion | bytes 2162688 | tf_op jit(solution)/shard_map/jit(_take)/gather | solution.py:46
  65.1 4.3 broadcast_in_dim.41
  73.4 20.9 %collective-permute-done = bf16[32,16,1024]{2,0,1:T(8,128)(2,1)S(1)} collective-permute-done((bf16[32,16,1024]{2,0,1:T(8,128)(2,1)S(1)}, bf16[32,16,1024]{2,0,1:T(8,128)(2,1)S(1)}, u32[]{:S(2)}, u32[]{:S(2)}) %collective-permute-start) | collective-permute-done | bytes 1048608 | tf_op jit(solution)/shard_map/ppermute | solution.py:18
  98.3 17.4 %collective-permute-done.2 = bf16[32,16,1024]{2,0,1:T(8,128)(2,1)S(1)} collective-permute-done((bf16[32,16,1024]{2,0,1:T(8,128)(2,1)S(1)}, bf16[32,16,1024]{2,0,1:T(8,128)(2,1)S(1)}, u32[]{:S(2)}, u32[]{:S(2)}) %collective-permute-start.2) | collective-permute-done | bytes 1048608 | tf_op jit(solution)/shard_map/ppermute | solution.py:18
  118.2 4.9 collective-permute-done.3
  123.1 13.0 %collective-permute-done.4 = bf16[32,16,1024]{2,0,1:T(8,128)(2,1)S(1)} collective-permute-done((bf16[32,16,1024]{2,0,1:T(8,128)(2,1)S(1)}, bf16[32,16,1024]{2,0,1:T(8,128)(2,1)S(1)}, u32[]{:S(2)}, u32[]{:S(2)}) %collective-permute-start.4) | collective-permute-done | bytes 1048608 | tf_op jit(solution)/shard_map/ppermute | solution.py:18
  155.8 5.7 %all-to-all-start = ((bf16[256,16,1024]{2,0,1:T(8,128)(2,1)}), bf16[256,16,1024]{2,0,1:T(8,128)(2,1)}, u32[]{:S(2)}, u32[]{:S(2)}) async-start(bf16[256,16,1024]{2,0,1:T(8,128)(2,1)} %constant_dynamic-update-slice_fusion), calls=%async_computation | async-start | bytes 16777216 | tf_op jit(solution)/shard_map/all_to_all | solution.py:48
  161.5 91.8 %all-to-all-done = bf16[256,16,1024]{2,0,1:T(8,128)(2,1)} async-done(((bf16[256,16,1024]{2,0,1:T(8,128)(2,1)}), bf16[256,16,1024]{2,0,1:T(8,128)(2,1)}, u32[]{:S(2)}, u32[]{:S(2)}) %all-to-all-start) | async-done | bytes 8388640 | tf_op jit(solution)/shard_map/all_to_all | solution.py:48
  253.3 8.0 %copy.20 = bf16[4,256,4,1024]{3,1,0,2:T(8,128)(2,1)} copy(bf16[4,256,4,1024]{3,1,2,0:T(8,128)(2,1)} %bitcast.14) | data formatting | bytes 16777216 | tf_op jit(solution)/shard_map/all_to_all | solution.py:48
  261.3 102.7 %while.20 = (s32[]{:T(128)}, bf16[16,512,1024]{2,1,0:T(8,128)(2,1)}, bf16[16,512,1024]{2,1,0:T(8,128)(2,1)}, s32[16]{0:T(128)S(1)}, bf16[4,1024,1024]{2,1,0:T(8,128)(2,1)}, /*index=5*/s32[]{:T(128)}, s32[]{:T(128)}, s32[]{:T(128)}) while((s32[]{:T(128)}, bf16[16,512,1024]{2,1,0:T(8,128)(2,1)}, bf16[16,512,1024]{2,1,0:T(8,128)(2,1)}, ...), condition=%wide.region_1.2_spmd, body=%wide.region_0.1_spmd.sunk | while | flops 1074266112 | bytes 4195463 | solution.py:59
  289.1 4.2 fusion.34
  301.9 4.3 fusion.34
  308.4 4.3 fusion.34
  334.1 4.2 fusion.34
  365.3 4.6 collective-permute-start.7
  375.9 4.4 collective-permute-done.8
  380.3 22.8 %pad_maximum_fusion = bf16[8704,1024]{1,0:T(8,128)(2,1)} fusion(bf16[256,1024]{1,0:T(8,128)(2,1)S(1)} %collective-permute-done.8, bf16[8192,1024]{1,0:T(8,128)(2,1)} %bitcast.68, bf16[256,1024]{1,0:T(8,128)(2,1)S(1)} %collective-permute-done.7), kind=kLoop, calls=%fused_computation.25 | loop fusion | flops 53477376 | bytes 35651584 | tf_op jit(solution)/shard_map/concatenate | solution.py:34
  403.1 122.8 %while.21 = (s32[]{:T(128)}, bf16[4,128,6,1024]{3,1,0,2:T(8,128)(2,1)}, bf16[4,128,6,24]{3,2,1,0:T(8,128)(2,1)S(1)}, s32[4,128,24]{2,1,0:T(8,128)S(1)}, bf16[8704,1024]{1,0:T(8,128)(2,1)}, /*index=5*/s32[]{:T(128)}) while((s32[]{:T(128)}, bf16[4,128,6,1024]{3,1,0,2:T(8,128)(2,1)}, bf16[4,128,6,24]{3,2,1,0:T(8,128)(2,1)S(1)}, ...), condition=%wide.region_3.4_spmd, body=%wide.region_2.3_spmd.sunk | while | flops 41711616 | bytes 23973456 | solution.py:73
  403.2 24.3 %gather_fusion = bf16[3072,1024]{1,0:T(8,128)(2,1)} fusion(bf16[8704,1024]{1,0:T(8,128)(2,1)} %get-tuple-element.187, s32[3072]{0:T(1024)S(1)} %broadcast_clamp_fusion.3), kind=kCustom, calls=%fused_computation.clone.1 | custom fusion | bytes 12595200 | tf_op jit(solution)/shard_map/while/body/eval_jaxpr/jit(_take)/gather | solution.py:67
  427.6 4.2 convert_bitcast_fusion.2
  433.9 24.3 %gather_fusion = bf16[3072,1024]{1,0:T(8,128)(2,1)} fusion(bf16[8704,1024]{1,0:T(8,128)(2,1)} %get-tuple-element.187, s32[3072]{0:T(1024)S(1)} %broadcast_clamp_fusion.3), kind=kCustom, calls=%fused_computation.clone.1 | custom fusion | bytes 12595200 | tf_op jit(solution)/shard_map/while/body/eval_jaxpr/jit(_take)/gather | solution.py:67
  464.6 24.3 %gather_fusion = bf16[3072,1024]{1,0:T(8,128)(2,1)} fusion(bf16[8704,1024]{1,0:T(8,128)(2,1)} %get-tuple-element.187, s32[3072]{0:T(1024)S(1)} %broadcast_clamp_fusion.3), kind=kCustom, calls=%fused_computation.clone.1 | custom fusion | bytes 12595200 | tf_op jit(solution)/shard_map/while/body/eval_jaxpr/jit(_take)/gather | solution.py:67
  489.0 4.2 convert_bitcast_fusion.2
  495.3 24.3 %gather_fusion = bf16[3072,1024]{1,0:T(8,128)(2,1)} fusion(bf16[8704,1024]{1,0:T(8,128)(2,1)} %get-tuple-element.187, s32[3072]{0:T(1024)S(1)} %broadcast_clamp_fusion.3), kind=kCustom, calls=%fused_computation.clone.1 | custom fusion | bytes 12595200 | tf_op jit(solution)/shard_map/while/body/eval_jaxpr/jit(_take)/gather | solution.py:67
  (89 shorter events, 121.1 us)
Async XLA Ops:
  70.7 23.6 %collective-permute-start = (bf16[32,16,1024]{2,0,1:T(8,128)(2,1)S(1)}, bf16[32,16,1024]{2,0,1:T(8,128)(2,1)S(1)}, u32[]{:S(2)}, u32[]{:S(2)}) collective-permute-start(bf16[32,16,1024]{2,0,1:T(8,128)(2,1)S(1)} %get-tuple-element.82), channel_id=1, source_target_pairs={{0,1},{1,2},{2,3},{3,4},{4,5},{5,6},{6,7},{7,0},{8,9},{9,10},{10,1... | collective-permute-start | bytes 3145736 | tf_op jit(solution)/shard_map/ppermute | solution.py:18
  73.4 24.9 %collective-permute-start.1 = (bf16[32,16,1024]{2,0,1:T(8,128)(2,1)S(1)}, bf16[32,16,1024]{2,0,1:T(8,128)(2,1)S(1)}, u32[]{:S(2)}, u32[]{:S(2)}) collective-permute-start(bf16[32,16,1024]{2,0,1:T(8,128)(2,1)S(1)} %get-tuple-element.82), channel_id=1, source_target_pairs={{0,7},{1,0},{2,1},{3,2},{4,3},{5,4},{6,5},{7,6},{8,15},{9,8},{10,9... | collective-permute-start | bytes 3145736 | tf_op jit(solution)/shard_map/ppermute | solution.py:21
  94.3 21.4 %collective-permute-start.2 = (bf16[32,16,1024]{2,0,1:T(8,128)(2,1)S(1)}, bf16[32,16,1024]{2,0,1:T(8,128)(2,1)S(1)}, u32[]{:S(2)}, u32[]{:S(2)}) collective-permute-start(bf16[32,16,1024]{2,0,1:T(8,128)(2,1)S(1)} %collective-permute-done), channel_id=1, source_target_pairs={{0,1},{1,2},{2,3},{3,4},{4,5},{5,6},{6,7},{7,0},{8,9},{9,10},{10,1... | collective-permute-start | bytes 3145736 | tf_op jit(solution)/shard_map/ppermute | solution.py:18
  98.3 24.8 %collective-permute-start.3 = (bf16[32,16,1024]{2,0,1:T(8,128)(2,1)S(1)}, bf16[32,16,1024]{2,0,1:T(8,128)(2,1)}, u32[]{:S(2)}, u32[]{:S(2)}) collective-permute-start(bf16[32,16,1024]{2,0,1:T(8,128)(2,1)S(1)} %collective-permute-done.1), channel_id=1, source_target_pairs={{0,7},{1,0},{2,1},{3,2},{4,3},{5,4},{6,5},{7,6},{8,15},{9,8},{10,9... | collective-permute-start | bytes 3145736 | tf_op jit(solution)/shard_map/ppermute | solution.py:21
  115.7 20.4 %copy-start = (bf16[32,16,1024]{2,0,1:T(8,128)(2,1)}, bf16[32,16,1024]{2,0,1:T(8,128)(2,1)S(1)}, u32[]{:S(2)}) copy-start(bf16[32,16,1024]{2,0,1:T(8,128)(2,1)S(1)} %collective-permute-done.2) | copy-start | bytes 3145732
  115.7 20.4 %collective-permute-start.4 = (bf16[32,16,1024]{2,0,1:T(8,128)(2,1)S(1)}, bf16[32,16,1024]{2,0,1:T(8,128)(2,1)S(1)}, u32[]{:S(2)}, u32[]{:S(2)}) collective-permute-start(bf16[32,16,1024]{2,0,1:T(8,128)(2,1)S(1)} %collective-permute-done.2), channel_id=1, source_target_pairs={{0,1},{1,2},{2,3},{3,4},{4,5},{5,6},{6,7},{7,0},{8,9},{9,10},{10,1... | collective-permute-start | bytes 3145736 | tf_op jit(solution)/shard_map/ppermute | solution.py:18
  123.1 24.4 %collective-permute-start.5 = (bf16[32,16,1024]{2,0,1:T(8,128)(2,1)}, bf16[32,16,1024]{2,0,1:T(8,128)(2,1)}, u32[]{:S(2)}, u32[]{:S(2)}) collective-permute-start(bf16[32,16,1024]{2,0,1:T(8,128)(2,1)} %collective-permute-done.3), channel_id=1, source_target_pairs={{0,7},{1,0},{2,1},{3,2},{4,3},{5,4},{6,5},{7,6},{8,15},{9,8},{10,9... | collective-permute-start | bytes 3145736 | tf_op jit(solution)/shard_map/ppermute | solution.py:21
  136.0 17.4 %collective-permute-start.6 = (bf16[32,16,1024]{2,0,1:T(8,128)(2,1)S(1)}, bf16[32,16,1024]{2,0,1:T(8,128)(2,1)}, u32[]{:S(2)}, u32[]{:S(2)}) collective-permute-start(bf16[32,16,1024]{2,0,1:T(8,128)(2,1)S(1)} %collective-permute-done.4), channel_id=1, source_target_pairs={{0,1},{1,2},{2,3},{3,4},{4,5},{5,6},{6,7},{7,0},{8,9},{9,10},{10,1... | collective-permute-start | bytes 3145736 | tf_op jit(solution)/shard_map/ppermute | solution.py:18
  155.8 97.5 %all-to-all-start = ((bf16[256,16,1024]{2,0,1:T(8,128)(2,1)}), bf16[256,16,1024]{2,0,1:T(8,128)(2,1)}, u32[]{:S(2)}, u32[]{:S(2)}) async-start(bf16[256,16,1024]{2,0,1:T(8,128)(2,1)} %constant_dynamic-update-slice_fusion), calls=%async_computation | async-start | bytes 16777216 | tf_op jit(solution)/shard_map/all_to_all | solution.py:48
  253.3 8.0 %copy-start.3 = (s32[16]{0:T(128)S(1)}, s32[16]{0:T(128)}, u32[]{:S(2)}) copy-start(s32[16]{0:T(128)} %param.13) | copy-start | bytes 196
  261.3 110.7 %copy-start.1 = (bf16[512,6,24]{0,2,1:T(8,128)(2,1)S(1)}, bf16[512,6,24]{0,2,1:T(8,128)(2,1)}, u32[]{:S(2)}) copy-start(bf16[512,6,24]{0,2,1:T(8,128)(2,1)} %param.15) | copy-start | bytes 442372
  261.3 111.5 %copy-start.2 = (s32[512,24]{0,1:T(8,128)S(1)}, s32[512,24]{0,1:T(8,128)}, u32[]{:S(2)}) copy-start(s32[512,24]{0,1:T(8,128)} %param.14) | copy-start | bytes 147460
  365.3 10.7 %collective-permute-start.7 = (bf16[256,1024]{1,0:T(8,128)(2,1)S(1)}, bf16[256,1024]{1,0:T(8,128)(2,1)S(1)}, u32[]{:S(2)}, u32[]{:S(2)}) collective-permute-start(bf16[256,1024]{1,0:T(8,128)(2,1)S(1)} %get-tuple-element.83), channel_id=1, source_target_pairs={{0,1},{1,2},{2,3},{3,4},{4,5},{5,6},{6,7},{8,9},{9,10},{10,11},{11... | collective-permute-start | bytes 1572872 | tf_op jit(solution)/shard_map/ppermute | solution.py:36
  369.8 10.5 %collective-permute-start.8 = (bf16[256,1024]{1,0:T(8,128)(2,1)S(1)}, bf16[256,1024]{1,0:T(8,128)(2,1)S(1)}, u32[]{:S(2)}, u32[]{:S(2)}) collective-permute-start(bf16[256,1024]{1,0:T(8,128)(2,1)S(1)} %get-tuple-element.84), channel_id=1, source_target_pairs={{1,0},{2,1},{3,2},{4,3},{5,4},{6,5},{7,6},{9,8},{10,9},{11,10},{12... | collective-permute-start | bytes 1572872 | tf_op jit(solution)/shard_map/ppermute | solution.py:38
